TPU v7x, 32 devices: a whole 2x2x4 slice. The times are simulated.
32 devices in a mesh: gx: 8 (over y, x, core), gy: 4 (over z).
Axes of the slice: x: 2, y: 2, z: 4, core: 2. Of those that a mesh axis runs over, the one named last changes fastest.
Arguments:
- cells: bfloat16 [1024, 256, 128], P('gx', 'gy'), may hold values from -6 to 6
- cotangent: bfloat16 [1024, 256, 128], P('gx', 'gy'), may hold values from -6 to 6
- lift_weight: bfloat16 [128, 512], replicated, may hold values from -0.5 to 0.5
- drop_weight: bfloat16 [512, 128], replicated, may hold values from -0.25 to 0.25
- xmode_weight: bfloat16 [2, 16, 128, 128], P(None, 'gx'), may hold values from -0.375 to 0.375
- ymode_weight: bfloat16 [2, 8, 128, 128], replicated, may hold values from -0.375 to 0.375
- coarse_weight: bfloat16 [128, 128], replicated, may hold values from -0.5 to 0.5
- coarse_mix: bfloat16 [16, 16], replicated, may hold values from -1.5 to 1.5
Outputs:
- cell_grad: bfloat16 [1024, 256, 128], P('gx', 'gy')
- lift_grad: float32 [128, 512], replicated
- drop_grad: float32 [512, 128], replicated
- xmode_grad: float32 [2, 16, 128, 128], P(None, 'gx')
- ymode_grad: float32 [2, 8, 128, 128], replicated
- coarse_weight_grad: float32 [128, 128], replicated
- coarse_mix_grad: float32 [16, 16], replicated
All inputs are finite; a program needn't handle non-finite values.
Results may differ from a plain program's by a relative error of at most 0.006.
Values sent between devices are 32-bit elements; how exact they have to be, the bound alone decides.
A program may use at most 128 MiB of HBM per device.

v0:
```python
import math
import jax
import jax.numpy as jnp
from jax import lax
from jax.sharding import PartitionSpec as P

MODES_X = 16
MODES_Y = 8
POOL = 16
gelu_scale = 0.7978845608028654
gelu_cubic = 0.044715
highest = lax.Precision.HIGHEST


def gelu_value(values):
    tangent = jnp.tanh(gelu_scale * (values + gelu_cubic * values * values * values))
    return 0.5 * values * (1.0 + tangent)


def gelu_slope(values):
    tangent = jnp.tanh(gelu_scale * (values + gelu_cubic * values * values * values))
    return 0.5 * (1.0 + tangent) + 0.5 * values * (1.0 - tangent * tangent) * gelu_scale * (
        1.0 + 3.0 * gelu_cubic * values * values
    )


def mode_basis(mode_count, length, offset, extent):
    frequency = jnp.arange(mode_count, dtype=jnp.int32)
    places = offset + jnp.arange(extent, dtype=jnp.int32)
    phase_index = frequency[:, None] * places[None, :] % length
    angles = phase_index.astype(jnp.float32) * (2.0 * math.pi / length)
    return jnp.concatenate([jnp.cos(angles), -jnp.sin(angles)], axis=0)


def mix_modes(spectrum, weights):

    def product(former, latter):
        return jnp.einsum("mrc,mcd->mrd", former, latter, precision=highest)

    real_out = product(spectrum[0], weights[0]) - product(spectrum[1], weights[1])
    imaginary_out = product(spectrum[0], weights[1]) + product(spectrum[1], weights[0])
    return jnp.stack([real_out, imaginary_out])


def mix_back(spectrum, gradient, weights):

    def contract_cells(former, latter):
        return jnp.einsum("mrc,mrd->mcd", former, latter, precision=highest)

    def contract_channels(former, latter):
        return jnp.einsum("mrd,mcd->mrc", former, latter, precision=highest)

    weight_real = contract_cells(spectrum[0], gradient[0]) + contract_cells(
        spectrum[1], gradient[1]
    )
    weight_imaginary = contract_cells(spectrum[0], gradient[1]) - contract_cells(
        spectrum[1], gradient[0]
    )
    spec_real = contract_channels(gradient[0], weights[0]) + contract_channels(
        gradient[1], weights[1]
    )
    spec_imaginary = contract_channels(gradient[1], weights[0]) - contract_channels(
        gradient[0], weights[1]
    )
    return (jnp.stack([weight_real, weight_imaginary]), jnp.stack([spec_real, spec_imaginary]))


def row_reduce(partial_spec):
    return lax.psum_scatter(partial_spec, "gx", scatter_dimension=1, tiled=True)


def row_return(owned_spec):
    return lax.all_gather(owned_spec, "gx", axis=1, tiled=True)


def column_reduce(partial_spec):
    return lax.psum_scatter(partial_spec, "gy", scatter_dimension=2, tiled=True)


def column_return(owned_spec):
    return lax.all_gather(owned_spec, "gy", axis=2, tiled=True)


def coarse_columns(coarse_block):
    return lax.all_gather(coarse_block, "gy", axis=1, tiled=True)


def upsample(coarse_field, row_count, column_count, channels):
    spread = jnp.broadcast_to(
        coarse_field[:, None, :, None, :],
        (row_count // POOL, POOL, column_count // POOL, POOL, channels),
    )
    return spread.reshape(row_count, column_count, channels)


def on_device(
    cells,
    cotangent,
    lift_weight,
    drop_weight,
    xmode_weight,
    ymode_weight,
    coarse_weight,
    coarse_mix,
):
    row_count, column_count, channels = cells.shape
    row_total = row_count * lax.axis_size("gx")
    column_total = column_count * lax.axis_size("gy")
    coarse_rows = row_count // POOL
    coarse_width = column_count // POOL
    row_basis = mode_basis(MODES_X, row_total, lax.axis_index("gx") * row_count, row_count)
    column_basis = mode_basis(
        MODES_Y, column_total, lax.axis_index("gy") * column_count, column_count
    )
    row_weight = xmode_weight.astype(jnp.float32)
    column_weight = ymode_weight.astype(jnp.float32)
    coarse_float = coarse_weight.astype(jnp.float32)
    mixing_float = coarse_mix.astype(jnp.float32)
    flat_cells = cells.reshape(row_count, column_count * channels)
    row_partial = jnp.dot(
        row_basis.astype(jnp.bfloat16), flat_cells, preferred_element_type=jnp.float32
    ) * (1.0 / math.sqrt(row_total))
    row_owned = row_reduce(row_partial.reshape(2, MODES_X, column_count, channels))
    row_mixed = row_return(mix_modes(row_owned, row_weight))
    row_field = jnp.dot(
        row_basis.T, row_mixed.reshape(2 * MODES_X, column_count * channels), precision=highest
    ) * (1.0 / math.sqrt(MODES_X))
    column_partial = jnp.einsum(
        "ry,xyc->rxc", column_basis.astype(jnp.bfloat16), cells, preferred_element_type=jnp.float32
    ) * (1.0 / math.sqrt(column_total))
    column_owned = column_reduce(column_partial.reshape(2, MODES_Y, row_count, channels))
    column_mixed = column_return(mix_modes(column_owned, column_weight))
    column_field = jnp.einsum(
        "ry,rxc->xyc",
        column_basis,
        column_mixed.reshape(2 * MODES_Y, row_count, channels),
        precision=highest,
    ) * (1.0 / math.sqrt(MODES_Y))
    pooled_own = cells.astype(jnp.float32).reshape(
        coarse_rows, POOL, coarse_width, POOL, channels
    ).sum(axis=(1, 3)) * (1.0 / POOL)
    pooled = coarse_columns(pooled_own)
    coarse_pre = jnp.einsum("ijc,cd->ijd", pooled, coarse_float, precision=highest)
    coarse_act = gelu_value(coarse_pre)
    column_offset = lax.axis_index("gy") * coarse_width
    mixing_rows = lax.dynamic_slice_in_dim(mixing_float, column_offset, coarse_width, 0)
    coarse_own = jnp.einsum("jk,ikc->ijc", mixing_rows, coarse_act, precision=highest)
    summed = (
        row_field.reshape(row_count, column_count, channels)
        + column_field
        + upsample(coarse_own, row_count, column_count, channels)
    )
    ffn_input = summed.reshape(row_count * column_count, channels).astype(jnp.bfloat16)
    hidden_before = jnp.dot(ffn_input, lift_weight, preferred_element_type=jnp.float32)
    hidden_after = gelu_value(hidden_before).astype(jnp.bfloat16)
    cotangent_rows = cotangent.reshape(row_count * column_count, channels)
    drop_partial = jnp.einsum(
        "nf,nc->fc", hidden_after, cotangent_rows, preferred_element_type=jnp.float32
    )
    after_grad = jnp.einsum(
        "nc,fc->nf", cotangent_rows, drop_weight, preferred_element_type=jnp.float32
    )
    before_grad = (after_grad * gelu_slope(hidden_before)).astype(jnp.bfloat16)
    lift_partial = jnp.einsum(
        "nc,nf->cf", ffn_input, before_grad, preferred_element_type=jnp.float32
    )
    summed_grad = jnp.einsum(
        "nf,cf->nc", before_grad, lift_weight, preferred_element_type=jnp.float32
    )
    summed_cells = summed_grad.reshape(row_count, column_count, channels)
    row_back_partial = jnp.dot(
        row_basis, summed_grad.reshape(row_count, column_count * channels), precision=highest
    ) * (1.0 / math.sqrt(MODES_X))
    row_back = row_reduce(row_back_partial.reshape(2, MODES_X, column_count, channels))
    row_weight_partial, row_spec_grad = mix_back(row_owned, row_back, row_weight)
    row_spec_full = row_return(row_spec_grad)
    row_cell_grad = jnp.dot(
        row_basis.T, row_spec_full.reshape(2 * MODES_X, column_count * channels), precision=highest
    ) * (1.0 / math.sqrt(row_total))
    column_back_partial = jnp.einsum(
        "ry,xyc->rxc", column_basis, summed_cells, precision=highest
    ) * (1.0 / math.sqrt(MODES_Y))
    column_back = column_reduce(column_back_partial.reshape(2, MODES_Y, row_count, channels))
    column_weight_partial, column_spec_grad = mix_back(column_owned, column_back, column_weight)
    column_spec_full = column_return(column_spec_grad)
    column_cell_grad = jnp.einsum(
        "ry,rxc->xyc",
        column_basis,
        column_spec_full.reshape(2 * MODES_Y, row_count, channels),
        precision=highest,
    ) * (1.0 / math.sqrt(column_total))
    coarse_grad_own = summed_cells.reshape(coarse_rows, POOL, coarse_width, POOL, channels).sum(
        axis=(1, 3)
    )
    coarse_grad = coarse_columns(coarse_grad_own)
    coarse_act_grad = jnp.einsum("jk,ijc->ikc", mixing_float, coarse_grad, precision=highest)
    mixing_partial = jnp.einsum("ijc,ikc->jk", coarse_grad, coarse_act, precision=highest)
    coarse_pre_grad = coarse_act_grad * gelu_slope(coarse_pre)
    coarse_weight_partial = jnp.einsum("ijc,ijd->cd", pooled, coarse_pre_grad, precision=highest)
    pre_grad_own = lax.dynamic_slice_in_dim(coarse_pre_grad, column_offset, coarse_width, 1)
    pooled_grad = jnp.einsum("ijd,cd->ijc", pre_grad_own, coarse_float, precision=highest) * (
        1.0 / POOL
    )
    cell_grad = (
        cotangent.astype(jnp.float32)
        + row_cell_grad.reshape(row_count, column_count, channels)
        + column_cell_grad
        + upsample(pooled_grad, row_count, column_count, channels)
    ).astype(jnp.bfloat16)
    xmode_grad = lax.psum(row_weight_partial, "gy")
    lift_grad, drop_grad, ymode_grad = lax.psum(
        (lift_partial, drop_partial, column_weight_partial), ("gx", "gy")
    )
    coarse_weight_grad, coarse_mix_grad = lax.psum((coarse_weight_partial, mixing_partial), "gx")
    return (
        cell_grad,
        lift_grad,
        drop_grad,
        xmode_grad,
        ymode_grad,
        coarse_weight_grad,
        coarse_mix_grad,
    )


def solution(mesh):
    in_specs = (
        P("gx", "gy", None),
        P("gx", "gy", None),
        P(),
        P(),
        P(None, "gx", None, None),
        P(),
        P(),
        P(),
    )
    out_specs = (P("gx", "gy", None), P(), P(), P(None, "gx", None, None), P(), P(), P())
    return jax.shard_map(
        on_device, mesh=mesh, in_specs=in_specs, out_specs=out_specs, check_vma=False
    )
```

profile of v0, /device:TPU:0, one launch (start us, length us, event | category | flops | bytes accessed | tf_op | source)
XLA Modules:
  0.0 478.8 jit_solution(4133987111560620458)
XLA Ops:
  8.2 3.1 fusion.17
  11.3 1.2 copy.53
  13.0 1.3 copy.33
  15.6 56.4 %all-reduce.11.cloned.1.call-done = f32[2,16,64,128]{3,2,1,0:T(8,128)} async-done(((f32[2,16,64,128]{3,2,1,0:T(8,128)}), f32[2,16,64,128]{3,2,1,0:T(8,128)}) %all-reduce.11.cloned.1.call-update) | async-done | bytes 1048592
  72.0 1.0 fusion.71
  73.0 1.0 fusion.34
  74.1 1.0 fusion.79
  75.1 1.0 fusion.35
  76.9 1.2 fusion.44
  78.1 1.2 fusion.27
  79.4 1.2 fusion.52
  80.6 1.2 fusion.28
  81.8 0.7 pad_maximum_fusion.1
  83.0 13.4 %all_gather.20 = f32[8,16,128]{2,0,1:T(8,128)S(1)} all-gather(f32[8,4,128]{2,0,1:T(8,128)S(1)} %copy_multiply_fusion), channel_id=1, replica_groups=mesh['gx'=8,'gy'=4] {'gy'}, dimensions={1}, use_global_device_ids=true | all-gather | bytes 81920 | tf_op jit(solution)/shard_map/all_gather | solution.py:85
  96.8 2.8 all-gather.5.cloned.1.call-done
  99.6 4.8 %fusion.13 = f32[16,8,64,128]{3,1,2,0:T(8,128)S(1)} fusion(f32[4,8,64,128]{3,2,1,0:T(8,128)} %bitcast.239, f32[16,128]{1,0:T(8,128)S(1)} %get-tuple-element.15, f32[16,128]{1,0:T(8,128)S(1)} %get-tuple-element.14), kind=kOutput, calls=%fused_computation.23 | convolution fusion | flops 403705856 | bytes 5259264 | tf_op jit(solution)/shard_map/dot_general | solution.py:125
  104.4 2.7 copy.55
  107.1 22.7 %all-gather.7.cloned.1.call-done = f32[2,8,128,128]{3,2,1,0:T(8,128)} async-done(((f32[2,8,32,128]{3,2,1,0:T(8,128)}), f32[2,8,128,128]{3,2,1,0:T(8,128)}) %all-gather.7.cloned.1.call-update) | async-done | bytes 1048592 | tf_op jit(solution)/shard_map/all_gather | solution.py:81
  130.2 1.7 copy-done.6
  132.0 5.5 %fusion.12 = bf16[128,64,128]{2,1,0:T(8,128)(2,1)S(1)} fusion(f32[128,64,128]{2,1,0:T(8,128)S(1)} %bitcast.232, f32[16,8,64,128]{3,2,1,0:T(8,128)S(1)} %copy-done.6, f32[16,128,128]{2,1,0:T(8,128)} %bitcast.240, f32[8,64]{1,0:T(8,128)S(1)} %get-tuple-element.13, f32[8,64]{1,0:T(8,128)S(1)} %get-tuple-element.12), kind=kOutput, calls=%fused_computation.21 | convolution fusion | flops 205521920 | bytes 11538432 | tf_op jit(solution)/shard_map/ry,rxc->xyc/dot_general | solution.py:133
  137.5 2.3 fusion.155
  139.8 12.1 %fusion.6 = bf16[8192,512]{1,0:T(8,128)(2,1)S(1)} fusion(f32[8192,512]{1,0:T(8,128)S(1)} %fusion.155, bf16[8192,128]{1,0:T(8,128)(2,1)S(1)} %bitcast.236, bf16[512,128]{1,0:T(8,128)(2,1)S(1)} %copy-done.15), kind=kOutput, calls=%fused_computation.8 | convolution fusion | flops 1153433600 | bytes 27394048 | tf_op jit(solution)/shard_map/nc,fc->nf/dot_general | solution.py:160
  151.9 3.3 copy-done.2
  155.2 4.3 fusion.156
  159.5 5.0 %reshape.90 = f32[128,8192]{1,0:T(8,128)} reshape(f32[8192,128]{1,0:T(8,128)} %fusion.156) | data formatting | bytes 8388608 | tf_op jit(solution)/shard_map/reshape | solution.py:172
  164.5 2.6 reduce_sum.19
  167.1 13.1 %all_gather.23 = f32[8,16,128]{2,0,1:T(8,128)S(1)} all-gather(f32[8,4,128]{2,0,1:T(8,128)S(1)} %copy.39), channel_id=1, replica_groups=mesh['gx'=8,'gy'=4] {'gy'}, dimensions={1}, use_global_device_ids=true | all-gather | bytes 81920 | tf_op jit(solution)/shard_map/all_gather | solution.py:85
  180.5 0.9 convolution_bitcast_fusion
  181.4 4.0 fusion.20
  185.4 1.2 copy.56
  186.6 3.8 fusion.21
  190.4 1.3 copy.37
  191.8 51.4 %all-reduce.15.cloned.1.call-done = (f32[2,16,64,128]{3,2,1,0:T(8,128)}, f32[128,128]{1,0:T(8,128)}) async-done(((f32[2,16,64,128]{3,2,1,0:T(8,128)}, f32[128,128]{1,0:T(8,128)}), (f32[2,16,64,128]{3,2,1,0:T(8,128)}, f32[128,128]{1,0:T(8,128)})) %all-reduce.15.cloned.1.call-update) | async-done | bytes 1114128
  243.2 1.1 fusion.74
  244.3 1.1 fusion.32
  245.3 1.1 fusion.76
  246.4 1.1 fusion.33
  248.3 1.4 fusion.47
  249.7 1.4 fusion.25
  251.1 1.4 fusion.49
  252.5 1.4 fusion.26
  254.0 0.7 pad_maximum_fusion.2
  254.8 10.9 %fusion.7 = f32[512,128]{1,0:T(8,128)} fusion(bf16[8192,128]{1,0:T(8,128)(2,1)} %bitcast.235, f32[8192,512]{1,0:T(8,128)} %copy-done.3), kind=kOutput, calls=%fused_computation.14 | convolution fusion | flops 1111490560 | bytes 19136512 | tf_op jit(solution)/shard_map/nf,nc->fc/dot_general | solution.py:157
  265.9 5.5 %fusion.157 = f32[128,512]{1,0:T(8,128)} fusion(bf16[8192,128]{1,0:T(8,128)(2,1)S(1)} %bitcast.228, bf16[8192,512]{1,0:T(8,128)(2,1)} %copy-done.2), kind=kOutput, calls=%fused_computation.215 | convolution fusion | flops 1073741824 | bytes 10747904 | tf_op jit(solution)/shard_map/nc,nf->cf/dot_general | solution.py:164
  271.3 1.3 fusion.86
  272.6 1.3 fusion.87
  273.9 1.3 fusion.29
  275.2 1.3 fusion.30
  277.2 1.0 fusion.62
  278.2 1.0 fusion.63
  279.3 1.0 fusion.23
  280.3 1.0 fusion.24
  281.3 1.1 pad_maximum_fusion
  282.6 13.7 %psum.47 = f32[16,16]{1,0:T(8,128)} all-reduce(f32[16,16]{1,0:T(8,128)S(1)} %convolution_bitcast_fusion.3), channel_id=1, replica_groups=mesh['gx'=8,'gy'=4] {'gx'}, use_global_device_ids=true, to_apply=%region_11.12 | all-reduce | flops 256 | bytes 2048 | tf_op jit(solution)/shard_map/psum | solution.py:214
  296.3 4.8 %fusion.14 = f32[16,8,64,128]{3,1,2,0:T(8,128)S(1)} fusion(f32[4,8,64,128]{3,2,1,0:T(8,128)} %bitcast.237, f32[16,128]{1,0:T(8,128)S(1)} %get-tuple-element.15, f32[16,128]{1,0:T(8,128)S(1)} %get-tuple-element.14), kind=kOutput, calls=%fused_computation.24 | convolution fusion | flops 403705856 | bytes 5259264 | tf_op jit(solution)/shard_map/dot_general | solution.py:177
  301.1 2.7 copy.58
  305.0 1.7 copy-done.5
  306.7 7.0 %fusion.10 = bf16[128,64,128]{2,1,0:T(8,128)(2,1)} fusion(f32[128,64,128]{2,1,0:T(8,128)S(1)} %bitcast.231, f32[16,8,64,128]{3,2,1,0:T(8,128)S(1)} %copy-done.5, bf16[128,64,128]{2,1,0:T(8,128)(2,1)S(1)} %copy-done.12, f32[16,128,128]{2,1,0:T(8,128)} %bitcast.238, f32[8,64]{1,0:T(8,128)S(1)} %get-tuple-element.13, f32[8,64]{1,0:T(8,128)S(1)} %get-tuple-element.12), kind=kOutput, calls=%fused_computation.18 | convolution fusion | flops 207619072 | bytes 13635584 | tf_op jit(solution)/shard_map/ry,rxc->xyc/dot_general | solution.py:186
  313.7 10.4 %all-reduce.9.cloned.1.call-done = f32[2,2,128,128]{3,2,1,0:T(8,128)} async-done(((f32[2,2,128,128]{3,2,1,0:T(8,128)}), f32[2,2,128,128]{3,2,1,0:T(8,128)}) %all-reduce.9.cloned.1.call-update) | async-done | bytes 262160 | tf_op jit(solution)/shard_map/psum | solution.py:210
  324.1 138.9 %all-reduce.13.cloned.1.call-done = (f32[128,512]{1,0:T(8,128)}, f32[512,128]{1,0:T(8,128)}, f32[2,8,128,128]{3,2,1,0:T(8,128)}) async-done(((f32[128,512]{1,0:T(8,128)}, f32[512,128]{1,0:T(8,128)}, f32[2,8,128,128]{3,2,1,0:T(8,128)}), (f32[128,512]{1,0:T(8,128)}, f32[512,128]{1,0:T(8,128)}, f32[2,8,128,128]{3,2,1,0:T(8,128)})) %all-reduce.13.cloned.1.call-update) | async-done | bytes 1572880 | tf_op jit(solution)/shard_map/psum | solution.py:211
  463.0 1.7 copy.95
  464.7 1.7 copy.96
  466.4 1.7 copy.97
  468.0 2.3 copy.98
  (79 shorter events, 7.5 us)
Async XLA Ops:
  8.0 129.4 %copy-start = (bf16[128,512]{1,0:T(8,128)(2,1)S(1)}, bf16[128,512]{1,0:T(8,128)(2,1)}, u32[]{:S(2)}) copy-start(bf16[128,512]{1,0:T(8,128)(2,1)} %param.10) | copy-start | bytes 393220
  8.0 4.6 copy-start.4
  8.0 64.0 %all-reduce.11.cloned.1.call-start = ((), (), s32[]{:S(2)}) async-start(), calls=%async_computation.9 | async-start | bytes 2097152
  12.4 1.9 copy-start.17
  12.4 59.6 %copy-start.10 = (bf16[2,2,128,128]{3,2,1,0:T(8,128)(2,1)S(1)}, bf16[2,2,128,128]{3,2,1,0:T(8,128)(2,1)}, u32[]{:S(2)}) copy-start(bf16[2,2,128,128]{3,2,1,0:T(8,128)(2,1)} %param.12) | copy-start | bytes 393220
  12.4 64.5 %copy-start.7 = (bf16[2,8,128,128]{3,2,1,0:T(8,128)(2,1)S(1)}, bf16[2,8,128,128]{3,2,1,0:T(8,128)(2,1)}, u32[]{:S(2)}) copy-start(bf16[2,8,128,128]{3,2,1,0:T(8,128)(2,1)} %param.13) | copy-start | bytes 1572868
  12.4 64.5 %reduce-scatter.9.cloned.1.call-start = ((), (), s32[]{:S(2)}) async-start(), calls=%async_computation.3 | async-start | bytes 1310720 | tf_op jit(solution)/shard_map/reduce_scatter | solution.py:77
  14.3 82.2 %copy-start.13 = (bf16[128,128]{1,0:T(8,128)(2,1)S(1)}, bf16[128,128]{1,0:T(8,128)(2,1)}, u32[]{:S(2)}) copy-start(bf16[128,128]{1,0:T(8,128)(2,1)} %param.14) | copy-start | bytes 98308
  14.3 82.3 %copy-start.16 = (bf16[16,16]{1,0:T(8,128)(2,1)S(1)}, bf16[16,16]{1,0:T(8,128)(2,1)}, u32[]{:S(2)}) copy-start(bf16[16,16]{1,0:T(8,128)(2,1)} %param.15) | copy-start | bytes 1540
  14.3 85.3 %all-gather.5.cloned.1.call-start = ((), (), s32[]{:S(2)}) async-start(), calls=%async_computation.2 | async-start | bytes 1179648 | tf_op jit(solution)/shard_map/all_gather | solution.py:73
  76.8 52.9 %all-gather.7.cloned.1.call-start = ((), (), s32[]{:S(2)}) async-start(), calls=%async_computation.4 | async-start | bytes 1310720 | tf_op jit(solution)/shard_map/all_gather | solution.py:81
  82.6 160.6 %all-reduce.15.cloned.1.call-start = ((), (), s32[]{:S(2)}) async-start(), calls=%async_computation.11 | async-start | bytes 2228224
  129.8 2.2 copy-start.6
  137.5 2.4 copy-start.11
  137.5 2.4 copy-start.15
  139.8 12.1 %copy-start.3 = (f32[8192,512]{1,0:T(8,128)}, f32[8192,512]{1,0:T(8,128)S(1)}, u32[]{:S(2)}) copy-start(f32[8192,512]{1,0:T(8,128)S(1)} %fusion.155) | copy-start | bytes 50331652
  151.9 3.3 copy-start.2
  186.5 61.7 %reduce-scatter.11.cloned.1.call-start = ((), (), s32[]{:S(2)}) async-start(), calls=%async_computation.6 | async-start | bytes 1310720 | tf_op jit(solution)/shard_map/reduce_scatter | solution.py:77
  191.8 104.5 %all-gather.9.cloned.1.call-start = ((), (), s32[]{:S(2)}) async-start(), calls=%async_computation.5 | async-start | bytes 1179648 | tf_op jit(solution)/shard_map/all_gather | solution.py:73
  248.2 56.3 %all-gather.11.cloned.1.call-start = ((), (), s32[]{:S(2)}) async-start(), calls=%async_computation.7 | async-start | bytes 1310720 | tf_op jit(solution)/shard_map/all_gather | solution.py:81
  254.7 69.4 %all-reduce.9.cloned.1.call-start = ((), (), s32[]{:S(2)}) async-start(), calls=%async_computation.8 | async-start | bytes 524288 | tf_op jit(solution)/shard_map/psum | solution.py:210
  265.8 11.4 %copy-start.8 = (f32[2,8,32,128]{3,2,1,0:T(8,128)S(1)}, f32[2,8,32,128]{3,2,1,0:T(8,128)}, u32[]{:S(2)}) copy-start(f32[2,8,32,128]{3,2,1,0:T(8,128)} %reduce-scatter.9.cloned.1.call-done) | copy-start | bytes 786436
  265.9 11.4 %copy-start.9 = (f32[2,8,32,128]{3,2,1,0:T(8,128)S(1)}, f32[2,8,32,128]{3,2,1,0:T(8,128)}, u32[]{:S(2)}) copy-start(f32[2,8,32,128]{3,2,1,0:T(8,128)} %reduce-scatter.11.cloned.1.call-done) | copy-start | bytes 786436
  277.2 185.8 %all-reduce.13.cloned.1.call-start = ((), (), s32[]{:S(2)}) async-start(), calls=%async_computation.10 | async-start | bytes 3145728 | tf_op jit(solution)/shard_map/psum | solution.py:211
  301.1 3.9 copy-start.12
  304.5 2.2 copy-start.5
  306.7 163.6 %copy-start.14 = (f32[128,128]{1,0:T(8,128)S(1)}, f32[128,128]{1,0:T(8,128)}, u32[]{:S(2)}) copy-start(f32[128,128]{1,0:T(8,128)} %get-tuple-element.21) | copy-start | bytes 196612
  306.7 164.2 %copy-start.1 = (bf16[128,512]{1,0:T(8,128)(2,1)S(1)}, bf16[128,512]{1,0:T(8,128)(2,1)}, u32[]{:S(2)}) copy-start(bf16[128,512]{1,0:T(8,128)(2,1)} %param.10) | copy-start | bytes 393220
Sparse Core Ops, SparseCore 0:
  12.6 59.4 all-reduce.10
  76.9 22.6 all-gather.4
  101.8 27.9 all-gather.6
  186.7 56.4 all-reduce.14
  248.3 22.6 all-gather.8
  273.0 31.4 all-gather.10
Sparse Core Ops, SparseCore 1:
  15.8 29.9 reduce-scatter.8
  191.8 26.6 reduce-scatter.10
  277.3 46.8 all-reduce.8
  330.4 132.5 all-reduce.12
where the time goes:
time: 484 us; the launch traced here: 479 us
  waiting for transfers between devices  283 us (58%)
  matrix products  98.3 us (20%)
  blocking collectives  40.2 us (8%)
  local copies, waits for them, and re-layouts  31.6 us (7%)
  between operations  17.1 us (4%)
  other arithmetic  7.65 us (2%)
    psum x1, waiting for transfers between devices, on_device(): lax.psum((lift_partial, drop_partial, column_weight_partial), ('gx', 'gy'))  139 us
    unnamed x12, waiting for transfers between devices  108 us
    all_gather x2, blocking collectives, coarse_columns(): return lax.all_gather(coarse_block, 'gy', axis=1, tiled=True)  26.5 us
    all_gather x2, waiting for transfers between devices, column_return(): return lax.all_gather(owned_spec, 'gy', axis=2, tiled=True)  23.4 us
    unnamed x46, local copies, waits for them, and re-layouts  23 us
    psum x1, blocking collectives, on_device(): lax.psum((coarse_weight_partial, mixing_partial), 'gx')  13.7 us
    dot_general x1, matrix products, on_device(): jnp.einsum('nc,fc->nf', cotangent_rows, drop_weight, preferred_element_ty...  12.1 us
    dot_general x1, matrix products, on_device(): jnp.einsum('nf,nc->fc', hidden_after, cotangent_rows, preferred_element_t...  10.9 us
  transfers between devices with their start and end apart: 10, of which 7 were waited for; matrix products, arithmetic and copies ran while one was open for 17% of the time, Pallas kernels for 0%

commit v1 on v0

--- a/solution.py
+++ b/solution.py
@@ -209,7 +209,7 @@
     ).astype(jnp.bfloat16)
     xmode_grad = lax.psum(row_weight_partial, "gy")
     lift_grad, drop_grad, ymode_grad = lax.psum(
-        (lift_partial, drop_partial, column_weight_partial), ("gx", "gy")
+        lax.psum((lift_partial, drop_partial, column_weight_partial), "gy"), "gx"
     )
     coarse_weight_grad, coarse_mix_grad = lax.psum((coarse_weight_partial, mixing_partial), "gx")
     return (

time: 484 us -> 422 us (0.87)
  waiting for transfers between devices: 283 us -> 227 us
  matrix products: 98.3 us -> 91.1 us
    psum x1, waiting for transfers between devices: 139 us -> 40.8 us  [on_device(): lax.psum((lift_partial, drop_partial, column_weight_partial), 'gy')]
    all_gather x2, waiting for transfers between devices: 23.4 us -> 46.2 us  [column_return(): return lax.all_gather(owned_spec, 'gy', axis=2, tiled=True)]
    unnamed x12, waiting for transfers between devices: 108 us -> 126 us
    reduce_scatter x2, waiting for transfers between devices: 0.05 us -> 10.5 us  [column_reduce(): return lax.psum_scatter(partial_spec, 'gy', scatter_dimension=2, tiled=True)]
    psum x1, waiting for transfers between devices: 10.4 us -> 0.01 us  [on_device(): xmode_grad = lax.psum(row_weight_partial, 'gy')]
    unnamed x46 -> x54, local copies, waits for them, and re-layouts: 23 us -> 23.6 us
  transfers between devices with their start and end apart: 10 -> 10, of which waited for: 7 -> 8; matrix products, arithmetic and copies ran while one was open for 17% -> 17% of each run, Pallas kernels for 0% -> 0%
where the time goes in v1:
time: 422 us; the launch traced here: 417 us
  waiting for transfers between devices  227 us (54%)
  matrix products  91.1 us (22%)
  blocking collectives  40.8 us (10%)
  local copies, waits for them, and re-layouts  32.2 us (8%)
  between operations  17.3 us (4%)
  other arithmetic  7.63 us (2%)
    unnamed x12, waiting for transfers between devices  126 us
    all_gather x2, waiting for transfers between devices, column_return(): return lax.all_gather(owned_spec, 'gy', axis=2, tiled=True)  46.2 us
    psum x1, waiting for transfers between devices, on_device(): lax.psum((lift_partial, drop_partial, column_weight_partial), 'gy')  40.8 us
    all_gather x2, blocking collectives, coarse_columns(): return lax.all_gather(coarse_block, 'gy', axis=1, tiled=True)  27.5 us
    unnamed x54, local copies, waits for them, and re-layouts  23.6 us
    psum x1, blocking collectives, on_device(): lax.psum((coarse_weight_partial, mixing_partial), 'gx')  13.3 us
    dot_general x8, matrix products, contract_cells(): return jnp.einsum('mrc,mrd->mcd', former, latter, precision=highest)  12.7 us
    dot_general x1, matrix products, on_device(): jnp.einsum('nc,fc->nf', cotangent_rows, drop_weight, preferred_element_ty...  11.7 us
  transfers between devices with their start and end apart: 10, of which 8 were waited for; matrix products, arithmetic and copies ran while one was open for 17% of the time, Pallas kernels for 0%

profile of v1, /device:TPU:0, one launch (start us, length us, event | category | flops | bytes accessed | tf_op | source)
XLA Modules:
  0.0 416.8 jit_solution(14394584376802943580)
XLA Ops:
  8.2 3.1 fusion.17
  11.3 1.2 copy.53
  13.0 1.3 copy.33
  15.6 56.4 %all-reduce.11.cloned.1.call-done = f32[2,16,64,128]{3,2,1,0:T(8,128)} async-done(((f32[2,16,64,128]{3,2,1,0:T(8,128)}), f32[2,16,64,128]{3,2,1,0:T(8,128)}) %all-reduce.11.cloned.1.call-update) | async-done | bytes 1048592
  72.0 1.0 fusion.71
  73.0 1.0 fusion.34
  74.1 1.0 fusion.79
  75.1 1.0 fusion.35
  76.9 1.2 fusion.44
  78.1 1.2 fusion.27
  79.4 1.2 fusion.52
  80.6 1.2 fusion.28
  81.8 0.7 pad_maximum_fusion.1
  83.0 13.6 %all_gather.20 = f32[8,16,128]{2,0,1:T(8,128)S(1)} all-gather(f32[8,4,128]{2,0,1:T(8,128)S(1)} %copy_multiply_fusion), channel_id=1, replica_groups=mesh['gx'=8,'gy'=4] {'gy'}, dimensions={1}, use_global_device_ids=true | all-gather | bytes 81920 | tf_op jit(solution)/shard_map/all_gather | solution.py:85
  97.0 2.6 all-gather.5.cloned.1.call-done
  99.6 4.8 %fusion.13 = f32[16,8,64,128]{3,1,2,0:T(8,128)S(1)} fusion(f32[4,8,64,128]{3,2,1,0:T(8,128)} %bitcast.239, f32[16,128]{1,0:T(8,128)S(1)} %get-tuple-element.18, f32[16,128]{1,0:T(8,128)S(1)} %get-tuple-element.17), kind=kOutput, calls=%fused_computation.23 | convolution fusion | flops 403705856 | bytes 5259264 | tf_op jit(solution)/shard_map/dot_general | solution.py:125
  104.4 2.7 copy.55
  107.1 22.6 %all-gather.7.cloned.1.call-done = f32[2,8,128,128]{3,2,1,0:T(8,128)} async-done(((f32[2,8,32,128]{3,2,1,0:T(8,128)}), f32[2,8,128,128]{3,2,1,0:T(8,128)}) %all-gather.7.cloned.1.call-update) | async-done | bytes 1048592 | tf_op jit(solution)/shard_map/all_gather | solution.py:81
  130.2 1.7 copy-done.8
  132.0 5.5 %fusion.12 = bf16[128,64,128]{2,1,0:T(8,128)(2,1)S(1)} fusion(f32[128,64,128]{2,1,0:T(8,128)S(1)} %bitcast.232, f32[16,8,64,128]{3,2,1,0:T(8,128)S(1)} %copy-done.8, f32[16,128,128]{2,1,0:T(8,128)} %bitcast.240, f32[8,64]{1,0:T(8,128)S(1)} %get-tuple-element.16, f32[8,64]{1,0:T(8,128)S(1)} %get-tuple-element.15), kind=kOutput, calls=%fused_computation.21 | convolution fusion | flops 205521920 | bytes 11538432 | tf_op jit(solution)/shard_map/ry,rxc->xyc/dot_general | solution.py:133
  137.5 2.3 fusion.155
  139.8 11.7 %fusion.6 = bf16[8192,512]{1,0:T(8,128)(2,1)S(1)} fusion(f32[8192,512]{1,0:T(8,128)S(1)} %fusion.155, bf16[8192,128]{1,0:T(8,128)(2,1)S(1)} %bitcast.236, bf16[512,128]{1,0:T(8,128)(2,1)S(1)} %copy-done.19), kind=kOutput, calls=%fused_computation.8 | convolution fusion | flops 1153433600 | bytes 27394048 | tf_op jit(solution)/shard_map/nc,fc->nf/dot_general | solution.py:160
  151.6 2.3 fusion.156
  153.9 0.9 copy-done.2
  154.8 2.0 copy-done.3
  156.8 2.1 fusion.21
  158.9 1.3 copy.37
  160.3 5.5 %fusion.157 = f32[128,512]{1,0:T(8,128)} fusion(bf16[8192,128]{1,0:T(8,128)(2,1)S(1)} %bitcast.228, bf16[8192,512]{1,0:T(8,128)(2,1)} %copy-done.2), kind=kOutput, calls=%fused_computation.215 | convolution fusion | flops 1073741824 | bytes 10747904 | tf_op jit(solution)/shard_map/nc,nf->cf/dot_general | solution.py:164
  165.8 2.9 copy-done.5
  168.7 7.7 %fusion.7 = f32[512,128]{1,0:T(8,128)} fusion(bf16[8192,128]{1,0:T(8,128)(2,1)} %bitcast.235, f32[8192,512]{1,0:T(8,128)S(1)} %copy-done.5), kind=kOutput, calls=%fused_computation.14 | convolution fusion | flops 1111490560 | bytes 19136512 | tf_op jit(solution)/shard_map/nf,nc->fc/dot_general | solution.py:157
  176.4 10.5 %reduce-scatter.11.cloned.1.call-done = f32[2,8,32,128]{3,2,1,0:T(8,128)} async-done(((f32[2,8,128,128]{3,2,1,0:T(8,128)}), f32[2,8,32,128]{3,2,1,0:T(8,128)}) %reduce-scatter.11.cloned.1.call-update) | async-done | bytes 262160 | tf_op jit(solution)/shard_map/reduce_scatter | solution.py:77
  186.9 1.9 fusion.62
  188.8 1.9 fusion.63
  190.7 1.9 fusion.23
  192.6 1.9 fusion.24
  194.5 1.0 pad_maximum_fusion
  195.9 4.9 %reshape.90 = f32[128,8192]{1,0:T(8,128)} reshape(f32[8192,128]{1,0:T(8,128)} %copy-done.3) | data formatting | bytes 8388608 | tf_op jit(solution)/shard_map/reshape | solution.py:172
  200.8 2.6 reduce_sum.19
  203.4 4.0 fusion.20
  207.4 1.2 copy.56
  208.6 13.9 %all_gather.23 = f32[8,16,128]{2,0,1:T(8,128)S(1)} all-gather(f32[8,4,128]{2,0,1:T(8,128)S(1)} %copy.39), channel_id=1, replica_groups=mesh['gx'=8,'gy'=4] {'gy'}, dimensions={1}, use_global_device_ids=true | all-gather | bytes 81920 | tf_op jit(solution)/shard_map/all_gather | solution.py:85
  222.7 0.9 convolution_bitcast_fusion
  223.6 40.8 %all-reduce.15.cloned.1.call-done = (f32[128,512]{1,0:T(8,128)}, f32[512,128]{1,0:T(8,128)}, f32[2,8,128,128]{3,2,1,0:T(8,128)}) async-done(((f32[128,512]{1,0:T(8,128)}, f32[512,128]{1,0:T(8,128)}, f32[2,8,128,128]{3,2,1,0:T(8,128)}), (f32[128,512]{1,0:T(8,128)}, f32[512,128]{1,0:T(8,128)}, f32[2,8,128,128]{3,2,1,0:T(8,128)})) %all-reduce.15.cloned.1.call-update) | async-done | bytes 1572880 | tf_op jit(solution)/shard_map/psum | solution.py:212
  264.5 69.5 %all-reduce.13.cloned.1.call-done = (f32[2,16,64,128]{3,2,1,0:T(8,128)}, f32[128,512]{1,0:T(8,128)}, f32[512,128]{1,0:T(8,128)}, f32[2,8,128,128]{3,2,1,0:T(8,128)}, f32[128,128]{1,0:T(8,128)}) async-done(((f32[2,16,64,128]{3,2,1,0:T(8,128)}, f32[128,512]{1,0:T(8,128)}, f32[512,128]{1,0:T(8,128)}, f32[2,8,128,128]{3,2,1,0:T(8,128)}, f32[128,128]{1,0:T(8,128)}), (f32[2,16,64,128]{3,2,1,0:T(8,128)}, ...) | async-done | bytes 2686992
  333.9 1.1 fusion.74
  335.0 1.1 fusion.76
  336.1 1.1 fusion.32
  337.2 1.1 fusion.33
  341.1 0.7 pad_maximum_fusion.2
  342.3 13.3 %psum.71 = f32[16,16]{1,0:T(8,128)} all-reduce(f32[16,16]{1,0:T(8,128)S(1)} %convolution_bitcast_fusion.3), channel_id=1, replica_groups=mesh['gx'=8,'gy'=4] {'gx'}, use_global_device_ids=true, to_apply=%region_14.15 | all-reduce | flops 256 | bytes 2048 | tf_op jit(solution)/shard_map/psum | solution.py:214
  355.6 1.3 fusion.86
  356.9 1.3 fusion.87
  358.1 1.3 fusion.29
  359.4 1.3 fusion.30
  360.7 0.7 pad_maximum_fusion.3
  361.4 1.0 all-gather.9.cloned.1.call-done
  362.4 4.8 %fusion.14 = f32[16,8,64,128]{3,1,2,0:T(8,128)S(1)} fusion(f32[4,8,64,128]{3,2,1,0:T(8,128)} %bitcast.237, f32[16,128]{1,0:T(8,128)S(1)} %get-tuple-element.18, f32[16,128]{1,0:T(8,128)S(1)} %get-tuple-element.17), kind=kOutput, calls=%fused_computation.24 | convolution fusion | flops 403705856 | bytes 5259264 | tf_op jit(solution)/shard_map/dot_general | solution.py:177
  367.3 2.7 copy.58
  370.0 23.6 %all-gather.11.cloned.1.call-done = f32[2,8,128,128]{3,2,1,0:T(8,128)} async-done(((f32[2,8,32,128]{3,2,1,0:T(8,128)}), f32[2,8,128,128]{3,2,1,0:T(8,128)}) %all-gather.11.cloned.1.call-update) | async-done | bytes 1048592 | tf_op jit(solution)/shard_map/all_gather | solution.py:81
  394.0 1.7 copy-done.7
  395.8 7.0 %fusion.10 = bf16[128,64,128]{2,1,0:T(8,128)(2,1)} fusion(f32[128,64,128]{2,1,0:T(8,128)S(1)} %bitcast.231, f32[16,8,64,128]{3,2,1,0:T(8,128)S(1)} %copy-done.7, bf16[128,64,128]{2,1,0:T(8,128)(2,1)S(1)} %copy-done.14, f32[16,128,128]{2,1,0:T(8,128)} %bitcast.238, f32[8,64]{1,0:T(8,128)S(1)} %get-tuple-element.16, f32[8,64]{1,0:T(8,128)S(1)} %get-tuple-element.15), kind=kOutput, calls=%fused_computation.18 | convolution fusion | flops 207619072 | bytes 13635584 | tf_op jit(solution)/shard_map/ry,rxc->xyc/dot_general | solution.py:186
  402.8 0.7 copy.98
  404.2 1.7 copy.100
  405.9 2.3 copy.101
  (87 shorter events, 9.1 us)
Async XLA Ops:
  8.0 129.4 %copy-start = (bf16[128,512]{1,0:T(8,128)(2,1)S(1)}, bf16[128,512]{1,0:T(8,128)(2,1)}, u32[]{:S(2)}) copy-start(bf16[128,512]{1,0:T(8,128)(2,1)} %param.10) | copy-start | bytes 393220
  8.0 4.6 %copy-start.6 = (bf16[128,64,128]{2,1,0:T(8,128)(2,1)S(1)}, bf16[128,64,128]{2,1,0:T(8,128)(2,1)}, u32[]{:S(2)}) copy-start(bf16[128,64,128]{2,1,0:T(8,128)(2,1)} %param.8) | copy-start | bytes 6291460
  8.0 64.0 %all-reduce.11.cloned.1.call-start = ((), (), s32[]{:S(2)}) async-start(), calls=%async_computation.9 | async-start | bytes 2097152
  12.4 1.9 copy-start.21
  12.4 59.6 %copy-start.12 = (bf16[2,2,128,128]{3,2,1,0:T(8,128)(2,1)S(1)}, bf16[2,2,128,128]{3,2,1,0:T(8,128)(2,1)}, u32[]{:S(2)}) copy-start(bf16[2,2,128,128]{3,2,1,0:T(8,128)(2,1)} %param.12) | copy-start | bytes 393220
  12.4 64.5 %copy-start.9 = (bf16[2,8,128,128]{3,2,1,0:T(8,128)(2,1)S(1)}, bf16[2,8,128,128]{3,2,1,0:T(8,128)(2,1)}, u32[]{:S(2)}) copy-start(bf16[2,8,128,128]{3,2,1,0:T(8,128)(2,1)} %param.13) | copy-start | bytes 1572868
  12.4 64.5 %reduce-scatter.9.cloned.1.call-start = ((), (), s32[]{:S(2)}) async-start(), calls=%async_computation.3 | async-start | bytes 1310720 | tf_op jit(solution)/shard_map/reduce_scatter | solution.py:77
  14.3 82.3 %copy-start.17 = (bf16[128,128]{1,0:T(8,128)(2,1)S(1)}, bf16[128,128]{1,0:T(8,128)(2,1)}, u32[]{:S(2)}) copy-start(bf16[128,128]{1,0:T(8,128)(2,1)} %param.14) | copy-start | bytes 98308
  14.3 82.5 %copy-start.20 = (bf16[16,16]{1,0:T(8,128)(2,1)S(1)}, bf16[16,16]{1,0:T(8,128)(2,1)}, u32[]{:S(2)}) copy-start(bf16[16,16]{1,0:T(8,128)(2,1)} %param.15) | copy-start | bytes 1540
  14.3 85.3 %all-gather.5.cloned.1.call-start = ((), (), s32[]{:S(2)}) async-start(), calls=%async_computation.2 | async-start | bytes 1179648 | tf_op jit(solution)/shard_map/all_gather | solution.py:73
  76.8 52.9 %all-gather.7.cloned.1.call-start = ((), (), s32[]{:S(2)}) async-start(), calls=%async_computation.4 | async-start | bytes 1310720 | tf_op jit(solution)/shard_map/all_gather | solution.py:81
  82.6 104.3 %reduce-scatter.11.cloned.1.call-start = ((), (), s32[]{:S(2)}) async-start(), calls=%async_computation.6 | async-start | bytes 1310720 | tf_op jit(solution)/shard_map/reduce_scatter | solution.py:77
  129.8 2.2 copy-start.8
  137.5 2.4 copy-start.13
  137.5 2.4 copy-start.19
  139.8 11.7 %copy-start.4 = (f32[8192,512]{1,0:T(8,128)}, f32[8192,512]{1,0:T(8,128)S(1)}, u32[]{:S(2)}) copy-start(f32[8192,512]{1,0:T(8,128)S(1)} %fusion.155) | copy-start | bytes 50331652
  151.6 3.3 copy-start.2
  154.8 2.0 copy-start.3
  160.2 104.2 %all-reduce.15.cloned.1.call-start = ((), (), s32[]{:S(2)}) async-start(), calls=%async_computation.11 | async-start | bytes 3145728 | tf_op jit(solution)/shard_map/psum | solution.py:212
  160.3 8.4 %copy-start.5 = (f32[8192,512]{1,0:T(8,128)S(1)}, f32[8192,512]{1,0:T(8,128)}, u32[]{:S(2)}) copy-start(f32[8192,512]{1,0:T(8,128)} %copy-done.4) | copy-start | bytes 50331652
  168.7 18.2 %copy-start.10 = (f32[2,8,32,128]{3,2,1,0:T(8,128)S(1)}, f32[2,8,32,128]{3,2,1,0:T(8,128)}, u32[]{:S(2)}) copy-start(f32[2,8,32,128]{3,2,1,0:T(8,128)} %reduce-scatter.9.cloned.1.call-done) | copy-start | bytes 786436
  195.6 138.3 %all-reduce.13.cloned.1.call-start = ((), (), s32[]{:S(2)}) async-start(), calls=%async_computation.10 | async-start | bytes 5373952
  207.4 131.6 %copy-start.11 = (f32[2,8,32,128]{3,2,1,0:T(8,128)S(1)}, f32[2,8,32,128]{3,2,1,0:T(8,128)}, u32[]{:S(2)}) copy-start(f32[2,8,32,128]{3,2,1,0:T(8,128)} %reduce-scatter.11.cloned.1.call-done) | copy-start | bytes 786436
  264.4 98.0 %all-gather.9.cloned.1.call-start = ((), (), s32[]{:S(2)}) async-start(), calls=%async_computation.5 | async-start | bytes 1179648 | tf_op jit(solution)/shard_map/all_gather | solution.py:73
  339.0 54.6 %all-gather.11.cloned.1.call-start = ((), (), s32[]{:S(2)}) async-start(), calls=%async_computation.7 | async-start | bytes 1310720 | tf_op jit(solution)/shard_map/all_gather | solution.py:81
  341.9 61.0 %all-reduce.9.cloned.1.call-start = ((), (), s32[]{:S(2)}) async-start(), calls=%async_computation.8 | async-start | bytes 524288 | tf_op jit(solution)/shard_map/psum | solution.py:210
  367.3 26.8 %copy-start.14 = (bf16[128,64,128]{2,1,0:T(8,128)(2,1)S(1)}, bf16[128,64,128]{2,1,0:T(8,128)(2,1)}, u32[]{:S(2)}) copy-start(bf16[128,64,128]{2,1,0:T(8,128)(2,1)} %param.9) | copy-start | bytes 6291460
  393.6 2.2 copy-start.7
  395.8 7.1 %copy-start.16 = (f32[128,512]{1,0:T(8,128)S(1)}, f32[128,512]{1,0:T(8,128)}, u32[]{:S(2)}) copy-start(f32[128,512]{1,0:T(8,128)} %get-tuple-element.20) | copy-start | bytes 786436
  395.8 7.8 %copy-start.15 = (f32[512,128]{1,0:T(8,128)S(1)}, f32[512,128]{1,0:T(8,128)}, u32[]{:S(2)}) copy-start(f32[512,128]{1,0:T(8,128)} %get-tuple-element.21) | copy-start | bytes 786436
  395.8 12.4 %copy-start.18 = (f32[128,128]{1,0:T(8,128)S(1)}, f32[128,128]{1,0:T(8,128)}, u32[]{:S(2)}) copy-start(f32[128,128]{1,0:T(8,128)} %get-tuple-element.24) | copy-start | bytes 196612
  395.8 13.1 %copy-start.1 = (bf16[128,512]{1,0:T(8,128)(2,1)S(1)}, bf16[128,512]{1,0:T(8,128)(2,1)}, u32[]{:S(2)}) copy-start(bf16[128,512]{1,0:T(8,128)(2,1)} %param.10) | copy-start | bytes 393220
Sparse Core Ops, SparseCore 0:
  12.6 59.4 all-reduce.10
  76.9 22.6 all-gather.4
  101.8 27.9 all-gather.6
  195.7 68.6 all-reduce.14
  268.6 65.2 all-reduce.12
  339.1 23.3 all-gather.8
  364.6 28.9 all-gather.10
Sparse Core Ops, SparseCore 1:
  15.8 29.9 reduce-scatter.8
  160.3 26.5 reduce-scatter.10
  361.5 40.1 all-reduce.8
